TPU v7x, 256 devices: a whole 4x4x8 slice. The times are simulated.
256 devices in a mesh: dp: 8 (over x, core), space: 32 (over y, z).
Axes of the slice: x: 4, y: 4, z: 8, core: 2. Of those that a mesh axis runs over, the one named last changes fastest.
Arguments:
- features: bfloat16 [8, 262144, 128], P('dp', 'space'), may hold values from -6 to 6
- child_parent: int32 [8, 262144], P('dp', 'space'), may hold values from 0 to 65535, as said below
- child_code: int32 [8, 262144], P('dp', 'space'), may hold values from 0 to 7
- weight: bfloat16 [8, 128, 128], replicated, may hold values from -0.25 to 0.25
- out_grad: bfloat16 [8, 65536, 128], P('dp', 'space'), may hold values from -6 to 6
Outputs:
- parent_out: bfloat16 [8, 65536, 128], P('dp', 'space')
- feature_grad: bfloat16 [8, 262144, 128], P('dp', 'space')
- weight_grad: float32 [8, 128, 128], replicated
Inputs may be any that keep to these rules, and one draw needn't show every extreme that they name: Within one window, child_parent is nondecreasing along the 8192 rows of one device of space. Parent p lies on device p // 2048 of space; at most 512 rows of one device have their parent on one device, and on every device some device receives exactly 512. No two fine octants of a window share both parent and child_code.
All inputs are finite; a program needn't handle non-finite values.
Results may differ from a plain program's by a relative error of at most 0.001.
Values may be sent and summed in bfloat16 or wider, within the bound.
A program may use at most 128 MiB of HBM per device.

v0:
```python
import jax
import jax.numpy as jnp
from jax import lax
from jax.sharding import PartitionSpec as P


def gather_blocks(rows, starts, capacity):
    extended = jnp.concatenate([rows, jnp.zeros((capacity,) + rows.shape[1:], rows.dtype)], axis=0)

    def window(offset):
        return lax.dynamic_slice_in_dim(extended, offset, capacity, 0)

    return jax.vmap(window)(starts)


def spread_blocks(blocks, starts, row_count):
    capacity = blocks.shape[1]
    channels = blocks.shape[2]
    canvas = jnp.zeros((row_count + capacity, channels), blocks.dtype)
    numbers = lax.ScatterDimensionNumbers(
        update_window_dims=(1, 2), inserted_window_dims=(), scatter_dims_to_operand_dims=(0,)
    )
    placed = lax.scatter_add(canvas, starts[:, None], blocks, numbers)
    return placed[:row_count]


def per_device(features, child_parent, child_code, weight, out_grad):
    fine_rows = features[0]
    parents = child_parent[0]
    child_kinds = child_code[0]
    cotangent = out_grad[0]
    row_count = fine_rows.shape[0]
    par_rows = cotangent.shape[0]
    kinds_total = weight.shape[0]
    chan_in = weight.shape[1]
    chan_out = weight.shape[2]
    space_size = lax.axis_size("space")
    capacity = 2 * row_count // space_size
    owners = parents // par_rows
    local_slot = (parents - owners * par_rows) * kinds_total + child_kinds
    counts = jnp.sum((owners[:, None] == jnp.arange(space_size)[None, :]).astype(jnp.int32), axis=0)
    starts = jnp.cumsum(counts) - counts
    slot_lane = jnp.arange(capacity)
    live_mask = slot_lane[None, :] < counts[:, None]
    marker = kinds_total * par_rows
    slot_blocks = gather_blocks(local_slot[:, None], starts, capacity)[:, :, 0]
    send_slots = jnp.where(live_mask, slot_blocks, marker)
    block_rows = min(512, row_count)
    block_count = row_count // block_rows
    kind_onehot = (child_kinds[:, None] == jnp.arange(kinds_total)[None, :]).astype(jnp.bfloat16)
    weight_cat = jnp.transpose(weight, (1, 0, 2)).reshape(chan_in, kinds_total * chan_out)
    weight_back = jnp.transpose(weight, (2, 0, 1)).reshape(chan_out, kinds_total * chan_in)
    rows_blocked = fine_rows.reshape(block_count, block_rows, chan_in)
    onehot_blocked = kind_onehot.reshape(block_count, block_rows, kinds_total)

    def forward_block(packed):
        rows, onehot = packed
        widened = jnp.dot(rows, weight_cat, preferred_element_type=jnp.float32).reshape(
            block_rows, kinds_total, chan_out
        )
        return jnp.sum(widened * onehot.astype(jnp.float32)[:, :, None], axis=1)

    products = lax.map(forward_block, (rows_blocked, onehot_blocked)).reshape(row_count, chan_out)
    part_blocks = gather_blocks(products, starts, capacity)
    send_parts = jnp.where(live_mask[:, :, None], part_blocks, 0.0)
    recv_parts, recv_slots = (
        lax.all_to_all(send_parts, "space", split_axis=0, concat_axis=0, tiled=True),
        lax.all_to_all(send_slots, "space", split_axis=0, concat_axis=0, tiled=True),
    )
    recv_parent = recv_slots // kinds_total
    summed = (
        jnp.zeros((par_rows, chan_out), jnp.float32)
        .at[recv_parent.reshape(-1)]
        .add(recv_parts.reshape(-1, chan_out), mode="drop")
    )
    result = summed.astype(jnp.bfloat16)
    back_rows = jnp.take(cotangent, recv_parent, axis=0, mode="fill", fill_value=0)
    returned = lax.all_to_all(back_rows, "space", split_axis=0, concat_axis=0, tiled=True)
    child_cot = spread_blocks(returned, starts, row_count)
    cot_blocked = child_cot.reshape(block_count, block_rows, chan_out)

    def backward_block(carry, packed):
        rows, onehot, cot = packed
        widened = jnp.dot(cot, weight_back, preferred_element_type=jnp.float32).reshape(
            block_rows, kinds_total, chan_in
        )
        grads = jnp.sum(widened * onehot.astype(jnp.float32)[:, :, None], axis=1).astype(
            jnp.bfloat16
        )
        placed = (rows[:, None, :] * onehot[:, :, None]).reshape(block_rows, kinds_total * chan_in)
        carry = carry + lax.dot_general(
            placed, cot, (((0,), (0,)), ((), ())), preferred_element_type=jnp.float32
        )
        return (carry, grads)

    start_term = jnp.zeros((kinds_total * chan_in, chan_out), jnp.float32)
    weight_term, grad_blocks = lax.scan(
        backward_block, start_term, (rows_blocked, onehot_blocked, cot_blocked)
    )
    feature_grad = grad_blocks.reshape(row_count, chan_in)
    summed_terms = lax.psum(weight_term, ("dp", "space"))
    total_rows = row_count * space_size * lax.axis_size("dp")
    weight_grad = (summed_terms / jnp.sqrt(jnp.float32(total_rows))).reshape(
        kinds_total, chan_in, chan_out
    )
    return (result[None], feature_grad[None], weight_grad)


def solution(mesh):
    placed = (
        P("dp", "space", None),
        P("dp", "space"),
        P("dp", "space"),
        P(),
        P("dp", "space", None),
    )
    return jax.shard_map(
        per_device,
        mesh=mesh,
        in_specs=placed,
        out_specs=(P("dp", "space", None), P("dp", "space", None), P()),
        check_vma=False,
    )
```

profile of v0, /device:TPU:2, one launch (start us, length us, event | category | flops | bytes accessed | tf_op | source)
XLA Modules:
  0.0 933.6 jit_solution(17775273788267957217)
XLA Ops:
  9.6 42.1 %while.32 = (s32[]{:T(128)}, s32[8704,1]{0,1:T(1,128)S(1)}, s32[32,2]{0,1:T(2,128)S(1)}, s32[32,512,1]{1,2,0:T(1,128)S(1)}) while((s32[]{:T(128)}, s32[8704,1]{0,1:T(1,128)S(1)}, s32[32,2]{0,1:T(2,128)S(1)}, s32[32,512,1]{1,2,0:T(1,128)S(1)}) %tuple.98), condition=%wide.while_cond.clone, body=%wide.while_body.sunk.clone | while | flops 2 | bytes 4193 | solution.py:11
  52.4 11.5 %all-to-all-start = ((s32[32,1,512]{2,1,0:T(1,128)}), s32[32,1,512]{2,1,0:T(1,128)S(1)}, u32[]{:S(2)}, u32[]{:S(2)}) async-start(s32[32,1,512]{2,1,0:T(1,128)} %compare_select_fusion.2), calls=%async_computation | async-start | bytes 131072 | tf_op jit(solution)/shard_map/all_to_all | solution.py:68
  67.1 37.0 %while.31 = (s32[]{:T(128)}, f32[16,512,128]{2,1,0:T(8,128)}, bf16[16,512,128]{2,1,0:T(8,128)(2,1)}, bf16[128,1024]{0,1:T(8,128)(2,1)S(1)}, bf16[16,512,8]{1,2,0:T(8,128)(2,1)S(1)}) while((s32[]{:T(128)}, f32[16,512,128]{2,1,0:T(8,128)}, bf16[16,512,128]{2,1,0:T(8,128)(2,1)}, bf16[128,1024]{0,1:T(8,128)(2,1)S(1)}, ...), condition=%wide.region_4.5_spmd.clone, body=%wide.region_2.4_spmd.sunk.clone | while | flops 135204864 | bytes 1220689 | solution.py:63
  104.5 57.4 %gather_fusion = bf16[16384,128]{1,0:T(8,128)(2,1)} fusion(bf16[2048,128]{1,0:T(8,128)(2,1)S(1)} %bitcast.167, s32[16384]{0:T(1024)S(1)} %broadcast_clamp_fusion), kind=kCustom, calls=%fused_computation | custom fusion | bytes 8454144 | tf_op jit(solution)/shard_map/jit(_take)/gather | solution.py:77
  161.9 7.7 broadcast_select_fusion.1
  169.6 9.9 %all-to-all-start.2 = ((bf16[32,512,128]{2,1,0:T(8,128)(2,1)}), bf16[32,512,128]{2,1,0:T(8,128)(2,1)}, u32[]{:S(2)}, u32[]{:S(2)}) async-start(bf16[32,512,128]{2,1,0:T(8,128)(2,1)} %broadcast_select_fusion.1), calls=%async_computation.2 | async-start | bytes 8388608 | tf_op jit(solution)/shard_map/all_to_all | solution.py:78
  179.6 3.8 concatenate.12
  183.4 93.2 %while.33 = (s32[]{:T(128)}, f32[8704,128]{1,0:T(8,128)}, s32[32,2]{0,1:T(2,128)S(1)}, f32[32,512,128]{2,1,0:T(8,128)}) while((s32[]{:T(128)}, f32[8704,128]{1,0:T(8,128)}, s32[32,2]{0,1:T(2,128)S(1)}, f32[32,512,128]{2,1,0:T(8,128)}) %tuple.121), condition=%wide.while_cond.1.clone, body=%wide.while_body.1.sunk.clone | while | flops 2 | bytes 524893 | solution.py:11
  184.0 2.3 bitcast_dynamic-update-slice_fusion.14
  189.9 2.3 bitcast_dynamic-update-slice_fusion.14
  201.5 2.3 bitcast_dynamic-update-slice_fusion.14
  207.3 2.3 bitcast_dynamic-update-slice_fusion.14
  213.2 2.3 bitcast_dynamic-update-slice_fusion.14
  233.5 2.3 bitcast_dynamic-update-slice_fusion.14
  236.4 2.3 bitcast_dynamic-update-slice_fusion.14
  256.8 2.3 bitcast_dynamic-update-slice_fusion.14
  259.7 2.3 bitcast_dynamic-update-slice_fusion.14
  274.3 2.3 bitcast_dynamic-update-slice_fusion.14
  276.6 9.9 %broadcast_select_fusion = f32[32,512,128]{2,1,0:T(8,128)} fusion(f32[32,512,128]{2,1,0:T(8,128)} %get-tuple-element.86, pred[32,512]{1,0:T(8,128)(4,1)S(1)} %iota_compare_fusion.2), kind=kLoop, calls=%fused_computation.28 | loop fusion | flops 2097152 | bytes 16793600 | tf_op jit(solution)/shard_map/jit(_where)/select_n | solution.py:65
  286.5 10.0 %all-to-all-start.1 = ((f32[32,512,128]{2,1,0:T(8,128)}), f32[32,512,128]{2,1,0:T(8,128)}, u32[]{:S(2)}, u32[]{:S(2)}) async-start(f32[32,512,128]{2,1,0:T(8,128)} %broadcast_select_fusion), calls=%async_computation.1 | async-start | bytes 16777216 | tf_op jit(solution)/shard_map/all_to_all | solution.py:67
  296.9 177.2 %while.34 = (s32[]{:T(128)}, bf16[8704,128]{1,0:T(8,128)(2,1)S(1)}, s32[32]{0:T(128)S(1)}, bf16[32,512,128]{2,1,0:T(8,128)(2,1)}, s32[2]{0:T(128)S(1)}, /*index=5*/s32[1]{0:T(128)}) while((s32[]{:T(128)}, bf16[8704,128]{1,0:T(8,128)(2,1)S(1)}, s32[32]{0:T(128)S(1)}, bf16[32,512,128]{2,1,0:T(8,128)(2,1)}, s32[2]{0:T(128)S(1)}, ...), condition=%wide.while_cond.2.clone, body=%wide.while_body.2.sunk.clone | while | flops 327691 | bytes 655479 | solution.py:23
  475.6 102.7 %while.35 = (s32[]{:T(128)}, f32[1024,128]{1,0:T(8,128)S(1)}, bf16[16,512,128]{2,1,0:T(8,128)(2,1)}, bf16[16,512,128]{2,1,0:T(8,128)(2,1)}, bf16[16,512,8]{1,2,0...) while((s32[]{:T(128)}, f32[1024,128]{1,0:T(8,128)S(1)}, ...), condition=%wide.region_9.10_spmd.clone.clone, body=%wide.region_7.9_spmd.clone.sunk.clone | while | flops 270209024 | bytes 4530291 | solution.py:97
  579.5 256.6 %all-reduce.5.cloned.1.call-done = f32[1024,128]{1,0:T(8,128)} async-done(((f32[1024,128]{1,0:T(8,128)}), f32[1024,128]{1,0:T(8,128)}) %all-reduce.5.cloned.1.call-update) | async-done | bytes 524304 | tf_op jit(solution)/shard_map/psum | solution.py:101
  838.0 87.9 %scatter_custom_fusion = f32[2048,128]{1,0:T(8,128)S(1)} fusion(s32[16384]{0:T(1024)S(1)} %bitcast.182, f32[16384,128]{1,0:T(8,128)} %bitcast.17, f32[]{:T(128)} %constant.60.clone.1), kind=kCustom, calls=%fused_computation.33 | custom fusion | flops 2097152 | bytes 1049088 | tf_op jit(solution)/shard_map/scatter-add | solution.py:74
  (512 shorter events, 439.7 us)
Async XLA Ops:
  7.2 97.3 %copy-start = (bf16[1,2048,128]{2,1,0:T(8,128)(2,1)S(1)}, bf16[1,2048,128]{2,1,0:T(8,128)(2,1)}, u32[]{:S(2)}) copy-start(bf16[1,2048,128]{2,1,0:T(8,128)(2,1)} %param.13) | copy-start | bytes 1572868
  52.4 51.7 %all-to-all-start = ((s32[32,1,512]{2,1,0:T(1,128)}), s32[32,1,512]{2,1,0:T(1,128)S(1)}, u32[]{:S(2)}, u32[]{:S(2)}) async-start(s32[32,1,512]{2,1,0:T(1,128)} %compare_select_fusion.2), calls=%async_computation | async-start | bytes 131072 | tf_op jit(solution)/shard_map/all_to_all | solution.py:68
  104.1 57.8 %copy-start.2 = (bf16[16,512,8]{1,2,0:T(8,128)(2,1)}, bf16[16,512,8]{1,2,0:T(8,128)(2,1)S(1)}, u32[]{:S(2)}) copy-start(bf16[16,512,8]{1,2,0:T(8,128)(2,1)S(1)} %get-tuple-element.503) | copy-start | bytes 393220
  169.6 116.9 %all-to-all-start.2 = ((bf16[32,512,128]{2,1,0:T(8,128)(2,1)}), bf16[32,512,128]{2,1,0:T(8,128)(2,1)}, u32[]{:S(2)}, u32[]{:S(2)}) async-start(bf16[32,512,128]{2,1,0:T(8,128)(2,1)} %broadcast_select_fusion.1), calls=%async_computation.2 | async-start | bytes 8388608 | tf_op jit(solution)/shard_map/all_to_all | solution.py:78
  286.5 10.4 %copy-start.3 = (s32[2]{0:T(128)S(1)}, s32[2]{0:T(128)}, u32[]{:S(2)}) copy-start(s32[2]{0:T(128)} %constant.226) | copy-start | bytes 28
  286.5 551.5 %all-to-all-start.1 = ((f32[32,512,128]{2,1,0:T(8,128)}), f32[32,512,128]{2,1,0:T(8,128)}, u32[]{:S(2)}, u32[]{:S(2)}) async-start(f32[32,512,128]{2,1,0:T(8,128)} %broadcast_select_fusion), calls=%async_computation.1 | async-start | bytes 16777216 | tf_op jit(solution)/shard_map/all_to_all | solution.py:67
  296.5 539.6 %all-reduce.5.cloned.1.call-start = ((), (), s32[]{:S(2)}) async-start(), calls=%async_computation.3 | async-start | bytes 1048576 | tf_op jit(solution)/shard_map/psum | solution.py:101
  578.4 0.8 copy-start.1
Sparse Core Ops, SparseCore 0:
  579.3 256.7 all-reduce.4
where the time goes:
time: 940 us; the launch traced here: 934 us
  local copies, waits for them, and re-layouts  298 us (32%)
  waiting for transfers between devices  257 us (27%)
  other arithmetic  255 us (27%)
  matrix products  76.7 us (8%)
  starting transfers between devices  31.4 us (3%)
  between operations  14.2 us (2%)
    psum x1, waiting for transfers between devices, per_device(): summed_terms = lax.psum(weight_term, ('dp', 'space'))  257 us
    gather x192, local copies, waits for them, and re-layouts  135 us
    scatter-add x64, other arithmetic  119 us
    scatter-add x1, other arithmetic, per_device(): summed = jnp.zeros((par_rows, chan_out), jnp.float32).at[recv_parent.resh...  87.9 us
    scatter-add x64, local copies, waits for them, and re-layouts  57.6 us
    gather x1, local copies, waits for them, and re-layouts, per_device(): jnp.take(cotangent, recv_parent, axis=0, mode='fill', fill_value=0)  57.4 us
    dot_general x16, matrix products, backward_block(): jnp.dot(cot, weight_back, preferred_element_type=jnp.float32)  26.9 us
    dot_general x16, matrix products, forward_block(): jnp.dot(rows, weight_cat, preferred_element_type=jnp.float32)  25 us
  transfers between devices with their start and end apart: 4, of which 1 were waited for; matrix products, arithmetic and copies ran while one was open for 46% of the time, Pallas kernels for 0%

commit v1 on v0

--- a/solution.py
+++ b/solution.py
@@ -98,7 +98,7 @@
         backward_block, start_term, (rows_blocked, onehot_blocked, cot_blocked)
     )
     feature_grad = grad_blocks.reshape(row_count, chan_in)
-    summed_terms = lax.psum(weight_term, ("dp", "space"))
+    summed_terms = lax.psum(lax.psum(weight_term, "dp"), "space")
     total_rows = row_count * space_size * lax.axis_size("dp")
     weight_grad = (summed_terms / jnp.sqrt(jnp.float32(total_rows))).reshape(
         kinds_total, chan_in, chan_out

time: 940 us -> 897 us (0.954)
  waiting for transfers between devices: 257 us -> 219 us
    psum x1 -> x2, waiting for transfers between devices: 257 us -> 219 us  [per_device(): summed_terms = lax.psum(lax.psum(weight_term, 'dp'), 'space')]
  transfers between devices with their start and end apart: 4 -> 5, of which waited for: 1 -> 2; matrix products, arithmetic and copies ran while one was open for 46% -> 48% of each run, Pallas kernels for 0% -> 0%
where the time goes in v1:
time: 897 us; the launch traced here: 891 us
  local copies, waits for them, and re-layouts  299 us (33%)
  other arithmetic  249 us (28%)
  waiting for transfers between devices  219 us (24%)
  matrix products  76.6 us (9%)
  starting transfers between devices  31.5 us (4%)
  between operations  14.2 us (2%)
    psum x2, waiting for transfers between devices, per_device(): summed_terms = lax.psum(lax.psum(weight_term, 'dp'), 'space')  219 us
    gather x192, local copies, waits for them, and re-layouts  139 us
    scatter-add x64, other arithmetic  112 us
    scatter-add x1, other arithmetic, per_device(): summed = jnp.zeros((par_rows, chan_out), jnp.float32).at[recv_parent.resh...  87.9 us
    gather x1, local copies, waits for them, and re-layouts, per_device(): jnp.take(cotangent, recv_parent, axis=0, mode='fill', fill_value=0)  57.4 us
    scatter-add x64, local copies, waits for them, and re-layouts  54.5 us
    dot_general x16, matrix products, backward_block(): jnp.dot(cot, weight_back, preferred_element_type=jnp.float32)  26.9 us
    dot_general x16, matrix products, forward_block(): jnp.dot(rows, weight_cat, preferred_element_type=jnp.float32)  25 us
  transfers between devices with their start and end apart: 5, of which 2 were waited for; matrix products, arithmetic and copies ran while one was open for 48% of the time, Pallas kernels for 0%

profile of v1, /device:TPU:2, one launch (start us, length us, event | category | flops | bytes accessed | tf_op | source)
XLA Modules:
  0.0 890.8 jit_solution(13288253710115002579)
XLA Ops:
  9.6 42.1 %while.32 = (s32[]{:T(128)}, s32[8704,1]{0,1:T(1,128)S(1)}, s32[32,2]{0,1:T(2,128)S(1)}, s32[32,512,1]{1,2,0:T(1,128)S(1)}) while((s32[]{:T(128)}, s32[8704,1]{0,1:T(1,128)S(1)}, s32[32,2]{0,1:T(2,128)S(1)}, s32[32,512,1]{1,2,0:T(1,128)S(1)}) %tuple.98), condition=%wide.while_cond.clone, body=%wide.while_body.sunk.clone | while | flops 2 | bytes 4193 | solution.py:11
  52.4 11.5 %all-to-all-start = ((s32[32,1,512]{2,1,0:T(1,128)}), s32[32,1,512]{2,1,0:T(1,128)S(1)}, u32[]{:S(2)}, u32[]{:S(2)}) async-start(s32[32,1,512]{2,1,0:T(1,128)} %compare_select_fusion.2), calls=%async_computation | async-start | bytes 131072 | tf_op jit(solution)/shard_map/all_to_all | solution.py:68
  67.1 36.9 %while.31 = (s32[]{:T(128)}, f32[16,512,128]{2,1,0:T(8,128)}, bf16[16,512,128]{2,1,0:T(8,128)(2,1)}, bf16[128,1024]{0,1:T(8,128)(2,1)S(1)}, bf16[16,512,8]{1,2,0:T(8,128)(2,1)S(1)}) while((s32[]{:T(128)}, f32[16,512,128]{2,1,0:T(8,128)}, bf16[16,512,128]{2,1,0:T(8,128)(2,1)}, bf16[128,1024]{0,1:T(8,128)(2,1)S(1)}, ...), condition=%wide.region_4.5_spmd.clone, body=%wide.region_2.4_spmd.sunk.clone | while | flops 135204864 | bytes 1220689 | solution.py:63
  104.4 57.4 %gather_fusion = bf16[16384,128]{1,0:T(8,128)(2,1)} fusion(bf16[2048,128]{1,0:T(8,128)(2,1)S(1)} %bitcast.167, s32[16384]{0:T(1024)S(1)} %broadcast_clamp_fusion), kind=kCustom, calls=%fused_computation | custom fusion | bytes 8454144 | tf_op jit(solution)/shard_map/jit(_take)/gather | solution.py:77
  161.9 7.7 broadcast_select_fusion.1
  169.6 9.9 %all-to-all-start.2 = ((bf16[32,512,128]{2,1,0:T(8,128)(2,1)}), bf16[32,512,128]{2,1,0:T(8,128)(2,1)}, u32[]{:S(2)}, u32[]{:S(2)}) async-start(bf16[32,512,128]{2,1,0:T(8,128)(2,1)} %broadcast_select_fusion.1), calls=%async_computation.2 | async-start | bytes 8388608 | tf_op jit(solution)/shard_map/all_to_all | solution.py:78
  179.6 3.8 concatenate.12
  183.5 97.5 %while.33 = (s32[]{:T(128)}, f32[8704,128]{1,0:T(8,128)}, s32[32,2]{0,1:T(2,128)S(1)}, f32[32,512,128]{2,1,0:T(8,128)}) while((s32[]{:T(128)}, f32[8704,128]{1,0:T(8,128)}, s32[32,2]{0,1:T(2,128)S(1)}, f32[32,512,128]{2,1,0:T(8,128)}) %tuple.123), condition=%wide.while_cond.1.clone, body=%wide.while_body.1.sunk.clone | while | flops 2 | bytes 524893 | solution.py:11
  190.2 2.4 bitcast_dynamic-update-slice_fusion.14
  193.3 2.4 bitcast_dynamic-update-slice_fusion.14
  199.4 2.4 bitcast_dynamic-update-slice_fusion.14
  202.4 2.4 bitcast_dynamic-update-slice_fusion.14
  208.6 2.4 bitcast_dynamic-update-slice_fusion.14
  211.6 2.4 bitcast_dynamic-update-slice_fusion.14
  214.7 2.4 bitcast_dynamic-update-slice_fusion.14
  229.9 2.4 bitcast_dynamic-update-slice_fusion.14
  239.0 2.4 bitcast_dynamic-update-slice_fusion.14
  280.9 9.9 %broadcast_select_fusion = f32[32,512,128]{2,1,0:T(8,128)} fusion(f32[32,512,128]{2,1,0:T(8,128)} %get-tuple-element.86, pred[32,512]{1,0:T(8,128)(4,1)S(1)} %iota_compare_fusion.2), kind=kLoop, calls=%fused_computation.28 | loop fusion | flops 2097152 | bytes 16793600 | tf_op jit(solution)/shard_map/jit(_where)/select_n | solution.py:65
  290.9 10.0 %all-to-all-start.1 = ((f32[32,512,128]{2,1,0:T(8,128)}), f32[32,512,128]{2,1,0:T(8,128)}, u32[]{:S(2)}, u32[]{:S(2)}) async-start(f32[32,512,128]{2,1,0:T(8,128)} %broadcast_select_fusion), calls=%async_computation.1 | async-start | bytes 16777216 | tf_op jit(solution)/shard_map/all_to_all | solution.py:67
  301.3 167.8 %while.34 = (s32[]{:T(128)}, bf16[8704,128]{1,0:T(8,128)(2,1)S(1)}, s32[32]{0:T(128)S(1)}, bf16[32,512,128]{2,1,0:T(8,128)(2,1)}, s32[2]{0:T(128)S(1)}, /*index=5*/s32[1]{0:T(128)}) while((s32[]{:T(128)}, bf16[8704,128]{1,0:T(8,128)(2,1)S(1)}, s32[32]{0:T(128)S(1)}, bf16[32,512,128]{2,1,0:T(8,128)(2,1)}, s32[2]{0:T(128)S(1)}, ...), condition=%wide.while_cond.2.clone, body=%wide.while_body.2.sunk.clone | while | flops 327691 | bytes 655479 | solution.py:23
  470.6 102.7 %while.35 = (s32[]{:T(128)}, f32[1024,128]{1,0:T(8,128)S(1)}, bf16[16,512,128]{2,1,0:T(8,128)(2,1)}, bf16[16,512,128]{2,1,0:T(8,128)(2,1)}, bf16[16,512,8]{1,2,0...) while((s32[]{:T(128)}, f32[1024,128]{1,0:T(8,128)S(1)}, ...), condition=%wide.region_9.10_spmd.clone.clone, body=%wide.region_7.9_spmd.clone.sunk.clone | while | flops 270209024 | bytes 4530291 | solution.py:97
  574.2 65.4 %all-reduce.6.cloned.1.call-done = f32[1024,128]{1,0:T(8,128)} async-done(((f32[1024,128]{1,0:T(8,128)}), f32[1024,128]{1,0:T(8,128)}) %all-reduce.6.cloned.1.call-update) | async-done | bytes 524304 | tf_op jit(solution)/shard_map/psum | solution.py:101
  639.9 153.4 %all-reduce.8.cloned.1.call-done = f32[1024,128]{1,0:T(8,128)} async-done(((f32[1024,128]{1,0:T(8,128)}), f32[1024,128]{1,0:T(8,128)}) %all-reduce.8.cloned.1.call-update) | async-done | bytes 524304 | tf_op jit(solution)/shard_map/psum | solution.py:101
  795.2 87.9 %scatter_custom_fusion = f32[2048,128]{1,0:T(8,128)S(1)} fusion(s32[16384]{0:T(1024)S(1)} %bitcast.182, f32[16384,128]{1,0:T(8,128)} %bitcast.17, f32[]{:T(128)} %constant.60.clone.1), kind=kCustom, calls=%fused_computation.33 | custom fusion | flops 2097152 | bytes 1049088 | tf_op jit(solution)/shard_map/scatter-add | solution.py:74
  (515 shorter events, 436.4 us)
Async XLA Ops:
  7.2 97.3 %copy-start = (bf16[1,2048,128]{2,1,0:T(8,128)(2,1)S(1)}, bf16[1,2048,128]{2,1,0:T(8,128)(2,1)}, u32[]{:S(2)}) copy-start(bf16[1,2048,128]{2,1,0:T(8,128)(2,1)} %param.13) | copy-start | bytes 1572868
  52.4 51.6 %all-to-all-start = ((s32[32,1,512]{2,1,0:T(1,128)}), s32[32,1,512]{2,1,0:T(1,128)S(1)}, u32[]{:S(2)}, u32[]{:S(2)}) async-start(s32[32,1,512]{2,1,0:T(1,128)} %compare_select_fusion.2), calls=%async_computation | async-start | bytes 131072 | tf_op jit(solution)/shard_map/all_to_all | solution.py:68
  104.1 57.8 %copy-start.2 = (bf16[16,512,8]{1,2,0:T(8,128)(2,1)}, bf16[16,512,8]{1,2,0:T(8,128)(2,1)S(1)}, u32[]{:S(2)}) copy-start(bf16[16,512,8]{1,2,0:T(8,128)(2,1)S(1)} %get-tuple-element.507) | copy-start | bytes 393220
  169.6 121.3 %all-to-all-start.2 = ((bf16[32,512,128]{2,1,0:T(8,128)(2,1)}), bf16[32,512,128]{2,1,0:T(8,128)(2,1)}, u32[]{:S(2)}, u32[]{:S(2)}) async-start(bf16[32,512,128]{2,1,0:T(8,128)(2,1)} %broadcast_select_fusion.1), calls=%async_computation.2 | async-start | bytes 8388608 | tf_op jit(solution)/shard_map/all_to_all | solution.py:78
  290.9 10.4 %copy-start.3 = (s32[2]{0:T(128)S(1)}, s32[2]{0:T(128)}, u32[]{:S(2)}) copy-start(s32[2]{0:T(128)} %constant.226) | copy-start | bytes 28
  290.9 504.3 %all-to-all-start.1 = ((f32[32,512,128]{2,1,0:T(8,128)}), f32[32,512,128]{2,1,0:T(8,128)}, u32[]{:S(2)}, u32[]{:S(2)}) async-start(f32[32,512,128]{2,1,0:T(8,128)} %broadcast_select_fusion), calls=%async_computation.1 | async-start | bytes 16777216 | tf_op jit(solution)/shard_map/all_to_all | solution.py:67
  300.9 338.7 %all-reduce.6.cloned.1.call-start = ((), (), s32[]{:S(2)}) async-start(), calls=%async_computation.3 | async-start | bytes 1048576 | tf_op jit(solution)/shard_map/psum | solution.py:101
  573.3 0.8 copy-start.1
  574.1 219.2 %all-reduce.8.cloned.1.call-start = ((), (), s32[]{:S(2)}) async-start(), calls=%async_computation.4 | async-start | bytes 1048576 | tf_op jit(solution)/shard_map/psum | solution.py:101
Sparse Core Ops, SparseCore 0:
  574.2 65.2 all-reduce.5
  643.0 150.3 all-reduce.7
